TPU v7x, 128 devices: a whole 4x4x4 slice. The times are simulated.
128 devices in a mesh: seq: 64 (over x_lo, z, y, core), ch: 2 (over x_hi).
Axes of the slice: x: 4 (x_hi: 2, x_lo: 2; x = x_hi * 2 + x_lo), y: 4, z: 4, core: 2. Of those that a mesh axis runs over, the one named last changes fastest.
Arguments:
- inputs: bfloat16 [4, 16384, 1536], P(None, 'seq', 'ch'), may hold values from -6 to 6
- kernels: float32 [3, 3, 1536], P(None, None, 'ch'), may hold values from -3.5 to 3.5
- mixers: bfloat16 [3, 1536, 1536], P(None, None, 'ch'), may hold values from -0.15625 to 0.15625
- cotangent: bfloat16 [4, 16384, 1536], P(None, 'seq', 'ch'), may hold values from -6 to 6
Outputs:
- outputs: bfloat16 [4, 16384, 1536], P(None, 'seq', 'ch')
- input_grad: bfloat16 [4, 16384, 1536], P(None, 'seq', 'ch')
- mixer_grads: float32 [3, 1536, 1536], P(None, 'seq', 'ch')
All inputs are finite; a program needn't handle non-finite values.
Results may differ from a plain program's by a relative error of at most 0.0075.
Values may be sent and summed in bfloat16 or wider, within the bound.
A program may use at most 128 MiB of HBM per device.

v0:
```python
import math
import jax
import jax.numpy as jnp
from jax import lax
from jax.sharding import PartitionSpec as P

dilations = (2, 4, 8)


def padded_2(block, sides, width):
    for axis, dim in sides:
        count = lax.axis_size(axis)
        forward = [(i, i + 1) for i in range(count - 1)]
        backward = [(target, source) for source, target in forward]
        low = lax.ppermute(
            lax.slice_in_dim(block, block.shape[dim] - width, None, axis=dim), axis, forward
        )
        high = lax.ppermute(lax.slice_in_dim(block, 0, width, axis=dim), axis, backward)
        block = jnp.concatenate([low, block, high], axis=dim)
    return block


def gelu_exact(value):
    return 0.5 * value * (1.0 + jax.scipy.special.erf(value * 0.7071067811865476))


def gelu_slope(value):
    return (
        0.5 * (1.0 + jax.scipy.special.erf(value * 0.7071067811865476))
        + value * jnp.exp(-0.5 * value * value) * 0.3989422804014327
    )


def convolve(padded, kernel, width):
    length = padded.shape[1] - 2 * width
    wide = padded.astype(jnp.float32)
    return (
        kernel[0] * wide[:, 0:length]
        + kernel[1] * wide[:, width : width + length]
        + kernel[2] * wide[:, 2 * width : 2 * width + length]
    )


def mixing(center, act, mixer):
    seqs, length, chans = act.shape
    gathered = lax.all_gather(act.reshape(seqs * length, chans), "ch", axis=1, tiled=True)
    mixed = jnp.dot(gathered, mixer, preferred_element_type=jnp.float32)
    result = (center.astype(jnp.float32) + mixed.reshape(seqs, length, chans)).astype(jnp.bfloat16)
    return (gathered, result)


def on_device(inputs, kernels, mixers, cotangent):
    seqs, bins, chans = inputs.shape
    devices_seq = lax.axis_size("seq")
    saved = []
    current = inputs
    for block, width in enumerate(dilations):
        padded = padded_2(current, (("seq", 1),), width)
        pre = convolve(padded, kernels[block], width)
        act = gelu_exact(pre).astype(jnp.bfloat16)
        gathered, current = mixing(current, act, mixers[block])
        saved.append((pre, gathered))
    scale = 1.0 / math.sqrt(seqs * bins * devices_seq)
    grad_list = [None, None, None]
    upper = cotangent
    for block in (2, 1, 0):
        width = dilations[block]
        kernel = kernels[block]
        pre, gathered = saved[block]
        flat = upper.reshape(seqs * bins, chans)
        term = jnp.einsum("rj,cj->rc", flat, mixers[block], preferred_element_type=jnp.float32)
        back = lax.psum_scatter(term, "ch", scatter_dimension=1, tiled=True)
        slope = (back.reshape(seqs, bins, chans) * gelu_slope(pre)).astype(jnp.bfloat16)
        local_grad = (
            jnp.einsum("rc,rj->cj", gathered, flat, preferred_element_type=jnp.float32) * scale
        )
        grad_list[block] = local_grad
        padded = padded_2(slope, (("seq", 1),), width).astype(jnp.float32)
        lower = (
            upper.astype(jnp.float32)
            + kernel[0] * padded[:, 2 * width : 2 * width + bins]
            + kernel[1] * padded[:, width : width + bins]
            + kernel[2] * padded[:, 0:bins]
        )
        upper = lower.astype(jnp.bfloat16)
    mixer_grads = lax.psum_scatter(jnp.stack(grad_list), "seq", scatter_dimension=1, tiled=True)
    return (current, upper, mixer_grads)


def solution(mesh):
    placed = (P(None, "seq", "ch"), P(None, None, "ch"), P(None, None, "ch"), P(None, "seq", "ch"))
    return jax.shard_map(
        on_device,
        mesh=mesh,
        in_specs=placed,
        out_specs=(P(None, "seq", "ch"), P(None, "seq", "ch"), P(None, "seq", "ch")),
        check_vma=False,
    )
```

profile of v0, /device:TPU:0, one launch (start us, length us, event | category | flops | bytes accessed | tf_op | source)
XLA Modules:
  0.0 783.3 jit_solution(2955091546215567638)
XLA Ops:
  9.4 3.0 collective-permute-start
  18.2 57.2 %all-gather.4.cloned.1.call-done = bf16[1024,1536]{1,0:T(8,128)(2,1)} async-done(((bf16[1024,768]{1,0:T(8,128)(2,1)}), bf16[1024,1536]{1,0:T(8,128)(2,1)}) %all-gather.4.cloned.1.call-update) | async-done | bytes 3145744 | tf_op jit(solution)/shard_map/all_gather | solution.py:46
  75.4 5.2 add_convert_fusion.2
  81.9 3.0 collective-permute-start.2
  89.1 6.2 fusion.38
  95.4 48.2 %all-gather.6.cloned.1.call-done = bf16[1024,1536]{1,0:T(8,128)(2,1)} async-done(((bf16[1024,768]{1,0:T(8,128)(2,1)}), bf16[1024,1536]{1,0:T(8,128)(2,1)}) %all-gather.6.cloned.1.call-update) | async-done | bytes 3145744 | tf_op jit(solution)/shard_map/all_gather | solution.py:46
  143.5 5.2 add_convert_fusion.1
  150.1 3.0 collective-permute-start.4
  154.3 72.2 %reduce-scatter.5.cloned.1.call-done = f32[1024,768]{1,0:T(8,128)} async-done(((f32[1024,1536]{1,0:T(8,128)}), f32[1024,768]{1,0:T(8,128)}) %reduce-scatter.5.cloned.1.call-update) | async-done | bytes 3145744 | tf_op jit(solution)/shard_map/reduce_scatter | solution.py:72
  226.5 4.5 fusion.5
  232.5 3.0 collective-permute-start.6
  238.8 6.2 fusion.42
  245.1 3.2 multiply_convert_fusion
  248.5 83.9 %reduce-scatter.7.cloned.1.call-done = f32[1024,768]{1,0:T(8,128)} async-done(((f32[1024,1536]{1,0:T(8,128)}), f32[1024,768]{1,0:T(8,128)}) %reduce-scatter.7.cloned.1.call-update) | async-done | bytes 3145744 | tf_op jit(solution)/shard_map/reduce_scatter | solution.py:72
  336.6 3.0 collective-permute-start.8
  341.8 6.9 fusion.46
  348.8 6.7 multiply_bitcast_fusion.1
  355.5 27.4 %all-gather.8.cloned.1.call-done = bf16[1024,1536]{1,0:T(8,128)(2,1)} async-done(((bf16[1024,768]{1,0:T(8,128)(2,1)}), bf16[1024,1536]{1,0:T(8,128)(2,1)}) %all-gather.8.cloned.1.call-update) | async-done | bytes 3145744 | tf_op jit(solution)/shard_map/all_gather | solution.py:46
  382.9 7.4 multiply_bitcast_fusion
  390.3 4.3 multiply_bitcast_fusion.2
  394.6 11.1 %pad_maximum_fusion = f32[3,1536,768]{2,1,0:T(8,128)} fusion(f32[1,1536,768]{2,1,0:T(8,128)} %multiply_bitcast_fusion, f32[1,1536,768]{2,1,0:T(8,128)} %multiply_bitcast_fusion.1, f32[1,1536,768]{2,1,0:T(8,128)} %multiply_bitcast_fusion.2), kind=kLoop, calls=%fused_computation | loop fusion | flops 7077888 | bytes 28311552 | tf_op jit(solution)/shard_map/stack | solution.py:86
  405.7 60.0 %reduce-scatter.9.cloned.1.call-done = f32[1024,768]{1,0:T(8,128)} async-done(((f32[1024,1536]{1,0:T(8,128)}), f32[1024,768]{1,0:T(8,128)}) %reduce-scatter.9.cloned.1.call-update) | async-done | bytes 3145744 | tf_op jit(solution)/shard_map/reduce_scatter | solution.py:72
  473.0 5.3 add_convert_fusion
  482.1 294.4 %reduce-scatter.11.cloned.1.call-done = f32[3,24,768]{2,1,0:T(8,128)} async-done(((f32[3,1536,768]{2,1,0:T(8,128)}), f32[3,24,768]{2,1,0:T(8,128)}) %reduce-scatter.11.cloned.1.call-update) | async-done | bytes 221200 | tf_op jit(solution)/shard_map/reduce_scatter | solution.py:86
  (79 shorter events, 38.1 us)
Async XLA Ops:
  7.2 68.2 %all-gather.4.cloned.1.call-start = ((), (), s32[]{:S(2)}) async-start(), calls=%async_computation.4 | async-start | bytes 4718592 | tf_op jit(solution)/shard_map/all_gather | solution.py:46
  8.1 5.3 collective-permute-start.1
  9.4 4.0 collective-permute-start
  15.1 60.2 %copy-start.8 = (bf16[4,256,768]{2,1,0:T(8,128)(2,1)S(1)}, bf16[4,256,768]{2,1,0:T(8,128)(2,1)}, u32[]{:S(2)}) copy-start(bf16[4,256,768]{2,1,0:T(8,128)(2,1)} %param.4) | copy-start | bytes 4718596
  18.1 125.4 %all-gather.6.cloned.1.call-start = ((), (), s32[]{:S(2)}) async-start(), calls=%async_computation.5 | async-start | bytes 4718592 | tf_op jit(solution)/shard_map/all_gather | solution.py:46
  80.6 4.3 collective-permute-start.3
  81.9 3.9 collective-permute-start.2
  89.0 137.5 %reduce-scatter.5.cloned.1.call-start = ((), (), s32[]{:S(2)}) async-start(), calls=%async_computation.7 | async-start | bytes 9437184 | tf_op jit(solution)/shard_map/reduce_scatter | solution.py:72
  95.3 237.0 %reduce-scatter.7.cloned.1.call-start = ((), (), s32[]{:S(2)}) async-start(), calls=%async_computation.8 | async-start | bytes 9437184 | tf_op jit(solution)/shard_map/reduce_scatter | solution.py:72
  148.8 4.3 collective-permute-start.5
  150.1 3.9 collective-permute-start.4
  231.1 4.5 collective-permute-start.7
  232.5 3.9 collective-permute-start.6
  245.0 137.9 %all-gather.8.cloned.1.call-start = ((), (), s32[]{:S(2)}) async-start(), calls=%async_computation.6 | async-start | bytes 4718592 | tf_op jit(solution)/shard_map/all_gather | solution.py:46
  245.0 87.3 %copy-start.1 = (f32[4,256,768]{2,1,0:T(8,128)S(1)}, f32[4,256,768]{2,1,0:T(8,128)}, u32[]{:S(2)}) copy-start(f32[4,256,768]{2,1,0:T(8,128)} %get-tuple-element.15) | copy-start | bytes 9437188
  248.3 217.4 %reduce-scatter.9.cloned.1.call-start = ((), (), s32[]{:S(2)}) async-start(), calls=%async_computation.9 | async-start | bytes 9437184 | tf_op jit(solution)/shard_map/reduce_scatter | solution.py:72
  335.1 4.5 collective-permute-start.9
  336.6 3.9 collective-permute-start.8
  341.8 48.5 %copy-start.4 = (bf16[4,256,768]{2,1,0:T(8,128)(2,1)}, bf16[4,256,768]{2,1,0:T(8,128)(2,1)S(1)}, u32[]{:S(2)}) copy-start(bf16[4,256,768]{2,1,0:T(8,128)(2,1)S(1)} %fusion.23) | copy-start | bytes 4718596
  348.8 427.7 %reduce-scatter.11.cloned.1.call-start = ((), (), s32[]{:S(2)}) async-start(), calls=%async_computation.10 | async-start | bytes 14376960 | tf_op jit(solution)/shard_map/reduce_scatter | solution.py:86
  382.9 7.4 copy-start.11
  405.7 60.0 %copy-start = (f32[4,256,768]{2,1,0:T(8,128)S(1)}, f32[4,256,768]{2,1,0:T(8,128)}, u32[]{:S(2)}) copy-start(f32[4,256,768]{2,1,0:T(8,128)} %get-tuple-element.17) | copy-start | bytes 9437188
  468.6 9.7 %collective-permute-start.11 = (bf16[4,2,768]{2,1,0:T(2,128)(2,1)S(1)}, bf16[4,2,768]{2,1,0:T(2,128)(2,1)S(1)}, u32[]{:S(2)}, u32[]{:S(2)}) collective-permute-start(bf16[4,2,768]{2,1,0:T(2,128)(2,1)S(1)} %get-tuple-element.19), channel_id=1, source_target_pairs={{2,0},{4,2},{6,4},{8,6},{10,8},{12,10},{14,12},{16,14},{18,16},{20... | collective-permute-start | bytes 36872 | tf_op jit(solution)/shard_map/ppermute | solution.py:18
  470.1 8.2 %collective-permute-start.10 = (bf16[4,2,768]{2,1,0:T(2,128)(2,1)S(1)}, bf16[4,2,768]{2,1,0:T(2,128)(2,1)S(1)}, u32[]{:S(2)}, u32[]{:S(2)}) collective-permute-start(bf16[4,2,768]{2,1,0:T(2,128)(2,1)S(1)} %get-tuple-element.18), channel_id=1, source_target_pairs={{0,2},{2,4},{4,6},{6,8},{8,10},{10,12},{12,14},{14,16},{16,18},{18... | collective-permute-start | bytes 36872 | tf_op jit(solution)/shard_map/ppermute | solution.py:15
  (8 other events, 36.7 us)
Sparse Core Ops, SparseCore 0:
  18.2 57.0 all-gather.3
  89.2 54.3 all-gather.5
  146.0 80.5 reduce-scatter.4
  245.1 87.2 reduce-scatter.6
  334.4 48.4 all-gather.7
  385.1 80.5 reduce-scatter.8
  468.8 307.5 reduce-scatter.10
where the time goes:
time: 784 us; the launch traced here: 783 us
  waiting for transfers between devices  647 us (83%)
  matrix products  53.5 us (7%)
  other arithmetic  37.8 us (5%)
  starting transfers between devices  26.7 us (3%)
  between operations  14.5 us (2%)
    reduce_scatter x1, waiting for transfers between devices, on_device(): lax.psum_scatter(jnp.stack(grad_list), 'seq', scatter_dimension=1, tiled=...  294 us
    reduce_scatter x3, waiting for transfers between devices, on_device(): back = lax.psum_scatter(term, 'ch', scatter_dimension=1, tiled=True)  216 us
    all_gather x3, waiting for transfers between devices, mixing(): lax.all_gather(act.reshape(seqs * length, chans), 'ch', axis=1, tiled=True)  133 us
    dot_general x3, matrix products, on_device(): jnp.einsum('rj,cj->rc', flat, mixers[block], preferred_element_type=jnp.f...  19.3 us
    dot_general x3, matrix products, on_device(): jnp.einsum('rc,rj->cj', gathered, flat, preferred_element_type=jnp.float32)  18.4 us
    ppermute x6, starting transfers between devices, padded_2(): lax.ppermute(lax.slice_in_dim(block, block.shape[dim] - width, None, axis...  18 us
    dot_general x3, matrix products, mixing(): mixed = jnp.dot(gathered, mixer, preferred_element_type=jnp.float32)  15.8 us
  transfers between devices with their start and end apart: 19, of which 11 were waited for; matrix products, arithmetic and copies ran while one was open for 9% of the time, Pallas kernels for 0%

commit v1 on v0

--- a/solution.py
+++ b/solution.py
@@ -43,7 +43,11 @@
 
 def mixing(center, act, mixer):
     seqs, length, chans = act.shape
-    gathered = lax.all_gather(act.reshape(seqs * length, chans), "ch", axis=1, tiled=True)
+    part = act.reshape(seqs * length, chans)
+    devices = lax.axis_size("ch")
+    blocks = jnp.stack([part for _ in range(devices)])
+    blocks = lax.all_to_all(blocks, "ch", split_axis=0, concat_axis=0)
+    gathered = jnp.concatenate(blocks, axis=1)
     mixed = jnp.dot(gathered, mixer, preferred_element_type=jnp.float32)
     result = (center.astype(jnp.float32) + mixed.reshape(seqs, length, chans)).astype(jnp.bfloat16)
     return (gathered, result)

time: 784 us -> 752 us (0.959)
  waiting for transfers between devices: 647 us -> 461 us
  blocking collectives: 0 us -> 117 us
  local copies, waits for them, and re-layouts: 4.22 us -> 31 us
  starting transfers between devices: 26.7 us -> 36.2 us
    all_gather x3 -> x0, waiting for transfers between devices: 133 us -> none  [mixing(): lax.all_gather(act.reshape(seqs * length, chans), 'ch', axis=1, tiled=True)]
    all_to_all x0 -> x2, blocking collectives: none -> 117 us  [mixing(): blocks = lax.all_to_all(blocks, 'ch', split_axis=0, concat_axis=0)]
    reduce_scatter x3, waiting for transfers between devices: 216 us -> 102 us  [on_device(): back = lax.psum_scatter(term, 'ch', scatter_dimension=1, tiled=True)]
    all_to_all x0 -> x1, waiting for transfers between devices: none -> 62.1 us  [mixing(): blocks = lax.all_to_all(blocks, 'ch', split_axis=0, concat_axis=0)]
    dot_general x0 -> x3, local copies, waits for them, and re-layouts: none -> 14 us  [mixing(): mixed = jnp.dot(gathered, mixer, preferred_element_type=jnp.float32)]
  transfers between devices with their start and end apart: 19 -> 17, of which waited for: 11 -> 9; matrix products, arithmetic and copies ran while one was open for 9% -> 11% of each run, Pallas kernels for 0% -> 0%
where the time goes in v1:
time: 752 us; the launch traced here: 751 us
  waiting for transfers between devices  461 us (61%)
  blocking collectives  117 us (16%)
  matrix products  55.2 us (7%)
  other arithmetic  36.6 us (5%)
  starting transfers between devices  36.2 us (5%)
  local copies, waits for them, and re-layouts  31 us (4%)
  between operations  14.2 us (2%)
    reduce_scatter x1, waiting for transfers between devices, on_device(): lax.psum_scatter(jnp.stack(grad_list), 'seq', scatter_dimension=1, tiled=...  293 us
    all_to_all x2, blocking collectives, mixing(): blocks = lax.all_to_all(blocks, 'ch', split_axis=0, concat_axis=0)  117 us
    reduce_scatter x3, waiting for transfers between devices, on_device(): back = lax.psum_scatter(term, 'ch', scatter_dimension=1, tiled=True)  102 us
    all_to_all x1, waiting for transfers between devices, mixing(): blocks = lax.all_to_all(blocks, 'ch', split_axis=0, concat_axis=0)  62.1 us
    ppermute x6, starting transfers between devices, padded_2(): lax.ppermute(lax.slice_in_dim(block, block.shape[dim] - width, None, axis...  22.2 us
    dot_general x3, matrix products, on_device(): jnp.einsum('rj,cj->rc', flat, mixers[block], preferred_element_type=jnp.f...  19.8 us
    dot_general x3, matrix products, on_device(): jnp.einsum('rc,rj->cj', gathered, flat, preferred_element_type=jnp.float32)  18.5 us
    dot_general x3, matrix products, mixing(): mixed = jnp.dot(gathered, mixer, preferred_element_type=jnp.float32)  16.9 us
  transfers between devices with their start and end apart: 17, of which 9 were waited for; matrix products, arithmetic and copies ran while one was open for 11% of the time, Pallas kernels for 0%

profile of v1, /device:TPU:0, one launch (start us, length us, event | category | flops | bytes accessed | tf_op | source)
XLA Modules:
  0.0 751.0 jit_solution(9603362228798752897)
XLA Ops:
  7.2 7.4 fusion.41
  24.6 76.8 %all_to_all.15 = bf16[2,1024,768]{2,1,0:T(8,128)(2,1)S(1)} all-to-all(bf16[2,1024,768]{2,1,0:T(8,128)(2,1)S(1)} %pad_maximum_fusion.1), channel_id=1, replica_groups=mesh['seq'=64,'ch'=2] {'ch'}, dimensions={0} | all-to-all | bytes 6291456 | tf_op jit(solution)/shard_map/all_to_all | solution.py:49
  103.1 3.2 copy.27
  106.3 3.3 dot_general.33
  109.6 5.6 add_convert_fusion.2
  124.6 40.1 %all_to_all.16 = bf16[2,1024,768]{1,2,0:T(8,128)(2,1)S(1)} all-to-all(bf16[2,1024,768]{1,2,0:T(8,128)(2,1)S(1)} %pad_maximum_fusion.2), channel_id=1, replica_groups=mesh['seq'=64,'ch'=2] {'ch'}, dimensions={0} | all-to-all | bytes 6291456 | tf_op jit(solution)/shard_map/all_to_all | solution.py:49
  164.6 4.3 reshape.84
  168.9 5.7 add_convert_fusion.1
  176.0 3.9 collective-permute-start.4
  181.1 4.6 fusion.5
  187.1 6.2 collective-permute-start.6
  196.4 6.2 fusion.44
  202.7 95.2 %reduce-scatter.7.cloned.1.call-done = f32[1024,768]{1,0:T(8,128)} async-done(((f32[1024,1536]{1,0:T(8,128)}), f32[1024,768]{1,0:T(8,128)}) %reduce-scatter.7.cloned.1.call-update) | async-done | bytes 3145744 | tf_op jit(solution)/shard_map/reduce_scatter | solution.py:76
  308.5 6.1 fusion.48
  321.7 5.5 all-to-all-start.2
  330.4 7.2 multiply_bitcast_fusion.1
  337.6 62.1 %all-to-all-done.2 = bf16[2,1024,768]{1,2,0:T(8,128)(2,1)} async-done(((bf16[2,1024,768]{1,2,0:T(8,128)(2,1)}), bf16[2,1024,768]{1,2,0:T(8,128)(2,1)}, u32[]{:S(2)}, u32[]{:S(2)}) %all-to-all-start.2) | async-done | bytes 3145760 | tf_op jit(solution)/shard_map/all_to_all | solution.py:49
  399.7 7.1 multiply_bitcast_fusion
  406.8 4.2 multiply_bitcast_fusion.2
  411.0 11.1 %pad_maximum_fusion = f32[3,1536,768]{2,1,0:T(8,128)} fusion(f32[1,1536,768]{2,1,0:T(8,128)} %multiply_bitcast_fusion, f32[1,1536,768]{2,1,0:T(8,128)} %multiply_bitcast_fusion.1, f32[1,1536,768]{2,1,0:T(8,128)} %multiply_bitcast_fusion.2), kind=kLoop, calls=%fused_computation | loop fusion | flops 7077888 | bytes 28311552 | tf_op jit(solution)/shard_map/stack | solution.py:90
  422.1 6.4 reshape.85
  428.5 6.5 reduce-scatter.9.cloned.1.call-done
  442.3 5.5 add_convert_fusion
  451.5 293.0 %reduce-scatter.11.cloned.1.call-done = f32[3,24,768]{2,1,0:T(8,128)} async-done(((f32[3,1536,768]{2,1,0:T(8,128)}), f32[3,24,768]{2,1,0:T(8,128)}) %reduce-scatter.11.cloned.1.call-update) | async-done | bytes 221200 | tf_op jit(solution)/shard_map/reduce_scatter | solution.py:90
  (98 shorter events, 59.5 us)
Async XLA Ops:
  7.2 174.0 %reduce-scatter.5.cloned.1.call-start = ((), (), s32[]{:S(2)}) async-start(), calls=%async_computation.7 | async-start | bytes 9437184 | tf_op jit(solution)/shard_map/reduce_scatter | solution.py:76
  14.7 283.3 %reduce-scatter.7.cloned.1.call-start = ((), (), s32[]{:S(2)}) async-start(), calls=%async_computation.8 | async-start | bytes 9437184 | tf_op jit(solution)/shard_map/reduce_scatter | solution.py:76
  16.1 4.4 collective-permute-start.1
  17.4 3.9 collective-permute-start
  115.3 8.3 %copy-start.15 = (bf16[4,256,768]{2,1,0:T(8,128)(2,1)}, bf16[4,256,768]{2,1,0:T(8,128)(2,1)S(1)}, u32[]{:S(2)}) copy-start(bf16[4,256,768]{2,1,0:T(8,128)(2,1)S(1)} %add_convert_fusion.2) | copy-start | bytes 4718596
  115.3 4.3 collective-permute-start.3
  116.6 3.9 collective-permute-start.2
  174.7 5.2 collective-permute-start.5
  176.0 4.8 collective-permute-start.4
  185.7 8.8 %copy-start.17 = (bf16[4,256,768]{2,1,0:T(8,128)(2,1)S(1)}, bf16[4,256,768]{2,1,0:T(8,128)(2,1)}, u32[]{:S(2)}) copy-start(bf16[4,256,768]{2,1,0:T(8,128)(2,1)} %param.7) | copy-start | bytes 4718596
  185.7 7.6 %collective-permute-start.7 = (bf16[4,8,768]{2,1,0:T(8,128)(2,1)S(1)}, bf16[4,8,768]{2,1,0:T(8,128)(2,1)S(1)}, u32[]{:S(2)}, u32[]{:S(2)}) collective-permute-start(bf16[4,8,768]{2,1,0:T(8,128)(2,1)S(1)} %get-tuple-element.23), channel_id=1, source_target_pairs={{2,0},{4,2},{6,4},{8,6},{10,8},{12,10},{14,12},{16,14},{18,16},{20... | collective-permute-start | bytes 147464 | tf_op jit(solution)/shard_map/ppermute | solution.py:18
  187.1 7.0 collective-permute-start.6
  202.6 95.3 %copy-start.4 = (f32[4,256,768]{2,1,0:T(8,128)S(1)}, f32[4,256,768]{2,1,0:T(8,128)}, u32[]{:S(2)}) copy-start(f32[4,256,768]{2,1,0:T(8,128)} %get-tuple-element.15) | copy-start | bytes 9437188
  202.7 232.4 %reduce-scatter.9.cloned.1.call-start = ((), (), s32[]{:S(2)}) async-start(), calls=%async_computation.9 | async-start | bytes 9437184 | tf_op jit(solution)/shard_map/reduce_scatter | solution.py:76
  300.7 4.5 collective-permute-start.9
  302.2 3.9 collective-permute-start.8
  321.7 78.0 %all-to-all-start.2 = ((bf16[2,1024,768]{1,2,0:T(8,128)(2,1)}), bf16[2,1024,768]{1,2,0:T(8,128)(2,1)}, u32[]{:S(2)}, u32[]{:S(2)}) async-start(bf16[2,1024,768]{1,2,0:T(8,128)(2,1)} %pad_maximum_fusion.3), calls=%async_computation.2 | async-start | bytes 6291456 | tf_op jit(solution)/shard_map/all_to_all | solution.py:49
  327.2 417.3 %reduce-scatter.11.cloned.1.call-start = ((), (), s32[]{:S(2)}) async-start(), calls=%async_computation.10 | async-start | bytes 14376960 | tf_op jit(solution)/shard_map/reduce_scatter | solution.py:90
  330.4 69.3 %copy-start.18 = (bf16[4,256,768]{2,1,0:T(8,128)(2,1)S(1)}, bf16[4,256,768]{2,1,0:T(8,128)(2,1)}, u32[]{:S(2)}) copy-start(bf16[4,256,768]{2,1,0:T(8,128)(2,1)} %param.7) | copy-start | bytes 4718596
  422.1 12.9 %copy-start.2 = (f32[4,256,768]{2,1,0:T(8,128)S(1)}, f32[4,256,768]{2,1,0:T(8,128)}, u32[]{:S(2)}) copy-start(f32[4,256,768]{2,1,0:T(8,128)} %get-tuple-element.17) | copy-start | bytes 9437188
  435.0 7.3 copy-start.11
  435.0 7.3 copy-start.14
  437.9 9.9 %collective-permute-start.11 = (bf16[4,2,768]{2,1,0:T(2,128)(2,1)S(1)}, bf16[4,2,768]{2,1,0:T(2,128)(2,1)S(1)}, u32[]{:S(2)}, u32[]{:S(2)}) collective-permute-start(bf16[4,2,768]{2,1,0:T(2,128)(2,1)S(1)} %get-tuple-element.19), channel_id=1, source_target_pairs={{2,0},{4,2},{6,4},{8,6},{10,8},{12,10},{14,12},{16,14},{18,16},{20... | collective-permute-start | bytes 36872 | tf_op jit(solution)/shard_map/ppermute | solution.py:18
  439.2 8.6 %collective-permute-start.10 = (bf16[4,2,768]{2,1,0:T(2,128)(2,1)S(1)}, bf16[4,2,768]{2,1,0:T(2,128)(2,1)S(1)}, u32[]{:S(2)}, u32[]{:S(2)}) collective-permute-start(bf16[4,2,768]{2,1,0:T(2,128)(2,1)S(1)} %get-tuple-element.18), channel_id=1, source_target_pairs={{0,2},{2,4},{4,6},{6,8},{8,10},{10,12},{12,14},{14,16},{16,18},{18... | collective-permute-start | bytes 36872 | tf_op jit(solution)/shard_map/ppermute | solution.py:15
  (13 other events, 50.7 us)
Sparse Core Ops, SparseCore 0:
  14.8 117.2 reduce-scatter.4
  202.8 95.1 reduce-scatter.6
  314.8 120.1 reduce-scatter.8
  438.0 306.4 reduce-scatter.10
